TPU v7x, 32 devices: a whole 2x2x4 slice. The times are simulated.
32 devices in a mesh: row: 2 (over x), col: 16 (over z, y, core).
Axes of the slice: x: 2, y: 2, z: 4, core: 2. Of those that a mesh axis runs over, the one named last changes fastest.
Arguments:
- tokens: bfloat16 [4096, 1024], P(('row', 'col')), may hold values from -6 to 6
- variate_ids: int32 [4096], P(('row', 'col')), may hold values from 0 to 3
- time_ids: int32 [4096], P(('row', 'col')), may hold values from 0 to 1023
- lengths: int32 [2, 6], P('row'), may hold values from 1 to 8, 16 in all within a row
- deal: int32 [2, 16, 16], P('row', 'col'), may hold values from 0 to 15, each once within a row
- w_qkv: bfloat16 [1024, 3072], P(('row', 'col')), may hold values from -0.1875 to 0.1875
- w_out: bfloat16 [1024, 1024], P(('row', 'col')), may hold values from -3 to 3
- w_gate_up: bfloat16 [1024, 8192], P(('row', 'col')), may hold values from -0.1875 to 0.1875
- w_down: bfloat16 [4096, 1024], P(('row', 'col')), may hold values from -0.09375 to 0.09375
- gain_attn: bfloat16 [1024], P(('row', 'col')), may hold values from 0.5 to 1.5
- gain_ffn: bfloat16 [1024], P(('row', 'col')), may hold values from 0.5 to 1.5
- var_bias: float32 [2, 16], replicated, may hold values from -3 to 3
- cotangent: bfloat16 [4096, 1024], P(('row', 'col')), may hold values from -6 to 6
Outputs:
- output: bfloat16 [4096, 1024], P(('row', 'col'))
- grad_tokens: bfloat16 [4096, 1024], P(('row', 'col'))
- grad_w_qkv: float32 [1024, 3072], P(('row', 'col'))
- grad_w_out: float32 [1024, 1024], P(('row', 'col'))
- grad_w_gate_up: float32 [1024, 8192], P(('row', 'col'))
- grad_w_down: float32 [4096, 1024], P(('row', 'col'))
- grad_gain_attn: float32 [1024], P(('row', 'col'))
- grad_gain_ffn: float32 [1024], P(('row', 'col'))
- grad_var_bias: float32 [2, 16], replicated
All inputs are finite; a program needn't handle non-finite values.
Results may differ from a plain program's by a relative error of at most 0.018.
The roundings to bfloat16 on the way count: a program that leaves them out, or rounds other values in their place, can miss the bound.
Values may be sent and summed in bfloat16 or wider, within the bound.
A program may use at most 320 MiB of HBM per device.

v0:
```python
import math
import jax
import jax.numpy as jnp
from jax import lax
from jax.sharding import PartitionSpec as P

HEAD_DIM = 64
UNIT = 128
KEY_BLOCK = 1024
epsilon = 1e-05


def contract_rows(operand, factor):
    return lax.dot_general(
        operand, factor, (((0,), (0,)), ((), ())), preferred_element_type=jnp.float32
    )


def contract_cols(operand, factor):
    return lax.dot_general(
        operand, factor, (((1,), (1,)), ((), ())), preferred_element_type=jnp.float32
    )


def angles(time_ids):
    half_dim = HEAD_DIM // 2
    inverse_freq = jnp.exp(-math.log(10000.0) * jnp.arange(half_dim, dtype=jnp.float32) / half_dim)
    phases = time_ids.astype(jnp.float32)[:, None] * inverse_freq[None, :]
    return (jnp.cos(phases)[:, None, :], jnp.sin(phases)[:, None, :])


def rotate(tensor, cos_part, sin_part):
    half_dim = tensor.shape[-1] // 2
    former = tensor[..., :half_dim]
    latter = tensor[..., half_dim:]
    return jnp.concatenate(
        [former * cos_part - latter * sin_part, latter * cos_part + former * sin_part], axis=-1
    )


def unrotate(tensor, cos_part, sin_part):
    half_dim = tensor.shape[-1] // 2
    former = tensor[..., :half_dim]
    latter = tensor[..., half_dim:]
    return jnp.concatenate(
        [former * cos_part + latter * sin_part, latter * cos_part - former * sin_part], axis=-1
    )


def norm_scale(values):
    return lax.rsqrt(jnp.mean(values * values, axis=-1, keepdims=True) + epsilon)


def norm_back(d_normed, normed, scale):
    return scale * (d_normed - normed * jnp.mean(d_normed * normed, axis=-1, keepdims=True))


def score_weights(queries, query_seq, query_var, key_block, seq_block, var_block, var_bias):
    scores = (
        jnp.einsum("qhd,khd->hqk", queries, key_block, preferred_element_type=jnp.float32) * 0.125
    )
    matched = query_var[:, None] == var_block[None, :]
    scores = scores + jnp.where(
        matched[None], var_bias[0][:, None, None], var_bias[1][:, None, None]
    )
    within = query_seq[:, None] == seq_block[None, :]
    return (jnp.where(within[None], jnp.exp(scores), 0.0), matched)


def shards(
    tokens,
    variate_ids,
    time_ids,
    lengths,
    deal,
    w_qkv,
    w_out,
    w_gate_up,
    w_down,
    gain_attn,
    gain_ffn,
    var_bias,
    cotangent,
):
    tok_rows, model_width = tokens.shape
    n_col = lax.axis_size("col")
    col_index = lax.axis_index("col")
    piece_len = tok_rows // n_col
    head_count = model_width // HEAD_DIM
    bounds = jnp.cumsum(lengths[0]) * UNIT
    position = col_index * tok_rows + jnp.arange(tok_rows, dtype=jnp.int32)
    seq_own = jnp.sum((position[:, None] >= bounds[None, :]).astype(jnp.int32), axis=1)
    target = deal[0, 0]
    slots = jnp.arange(n_col, dtype=jnp.int32)
    inverse = jnp.sum(
        slots[:, None] * (target[:, None] == slots[None, :]).astype(jnp.int32), axis=0
    )
    send_rows = jnp.take(tokens.reshape(n_col, piece_len, model_width), inverse, axis=0)
    labels = jnp.stack(
        [
            seq_own.reshape(n_col, piece_len),
            variate_ids.reshape(n_col, piece_len),
            time_ids.reshape(n_col, piece_len),
        ],
        axis=1,
    )
    send_labels = jnp.take(labels, inverse, axis=0)
    got_rows, got_labels = (
        lax.all_to_all(send_rows, "col", split_axis=0, concat_axis=0, tiled=True),
        lax.all_to_all(send_labels, "col", split_axis=0, concat_axis=0, tiled=True),
    )
    inputs = got_rows.reshape(tok_rows, model_width).astype(jnp.float32)
    seq_q = got_labels[:, 0, :].reshape(tok_rows)
    var_q = got_labels[:, 1, :].reshape(tok_rows)
    cos_part, sin_part = angles(got_labels[:, 2, :].reshape(tok_rows))
    qkv_full, out_full, gate_up_full, down_full, gain_one, gain_two = (
        lax.all_gather(w_qkv, ("row", "col"), axis=0, tiled=True),
        lax.all_gather(w_out, ("row", "col"), axis=0, tiled=True),
        lax.all_gather(w_gate_up, ("row", "col"), axis=0, tiled=True),
        lax.all_gather(w_down, ("row", "col"), axis=0, tiled=True),
        lax.all_gather(gain_attn, ("row", "col"), axis=0, tiled=True),
        lax.all_gather(gain_ffn, ("row", "col"), axis=0, tiled=True),
    )
    scale_one = norm_scale(inputs)
    normed_one = inputs * scale_one
    scaled_one = (normed_one * gain_one.astype(jnp.float32)).astype(jnp.bfloat16)
    projected = jnp.dot(scaled_one, qkv_full, preferred_element_type=jnp.float32)
    shaped = projected.reshape(tok_rows, 3, head_count, HEAD_DIM)
    queries = rotate(shaped[:, 0], cos_part, sin_part).astype(jnp.bfloat16)
    key_own = (
        rotate(shaped[:, 1], cos_part, sin_part).astype(jnp.bfloat16).reshape(tok_rows, model_width)
    )
    value_own = projected[:, 2 * model_width :].astype(jnp.bfloat16)
    keys_all, values_all, seq_k, var_k = (
        lax.all_gather(key_own, "col", axis=0, tiled=True),
        lax.all_gather(value_own, "col", axis=0, tiled=True),
        lax.all_gather(seq_q, "col", axis=0, tiled=True),
        lax.all_gather(var_q, "col", axis=0, tiled=True),
    )
    group_size = keys_all.shape[0]
    stride = min(KEY_BLOCK, group_size)
    block_count = group_size // stride

    def split_blocks(key_rows, value_rows, key_seq, key_var):
        return (
            key_rows.reshape(block_count, stride, head_count, HEAD_DIM),
            value_rows.reshape(block_count, stride, head_count, HEAD_DIM),
            key_seq.reshape(block_count, stride),
            key_var.reshape(block_count, stride),
        )

    def forward_step(running, block_data):
        denominator, numerator = running
        key_block, value_block, seq_block, var_block = block_data
        weights = score_weights(queries, seq_q, var_q, key_block, seq_block, var_block, var_bias)[0]
        denominator = denominator + jnp.sum(weights, axis=-1)
        numerator = numerator + jnp.einsum(
            "hqk,khd->qhd",
            weights.astype(jnp.bfloat16),
            value_block,
            preferred_element_type=jnp.float32,
        )
        return ((denominator, numerator), None)

    (denominator, numerator), unused = lax.scan(
        forward_step,
        (
            jnp.zeros((head_count, tok_rows), jnp.float32),
            jnp.zeros((tok_rows, head_count, HEAD_DIM), jnp.float32),
        ),
        split_blocks(keys_all, values_all, seq_k, var_k),
    )
    attended = numerator / denominator.T[:, :, None]
    attn_low = attended.reshape(tok_rows, model_width).astype(jnp.bfloat16)
    hidden_state = inputs + jnp.dot(attn_low, out_full, preferred_element_type=jnp.float32)
    scale_two = norm_scale(hidden_state)
    normed_two = hidden_state * scale_two
    scaled_two = (normed_two * gain_two.astype(jnp.float32)).astype(jnp.bfloat16)
    gate_up = jnp.dot(scaled_two, gate_up_full, preferred_element_type=jnp.float32)
    hidden_units = gate_up_full.shape[1] // 2
    gate_part = gate_up[:, :hidden_units]
    upper_part = gate_up[:, hidden_units:]
    sigmoid_gate = jax.nn.sigmoid(gate_part)
    active = gate_part * sigmoid_gate
    inner_act = (active * upper_part).astype(jnp.bfloat16)
    ffn_branch = jnp.dot(inner_act, down_full, preferred_element_type=jnp.float32)
    output = (hidden_state + ffn_branch).astype(jnp.bfloat16)
    qkv_back, out_back, gate_up_back, down_back, gain_one_back, gain_two_back = (
        lax.all_gather(w_qkv, ("row", "col"), axis=0, tiled=True),
        lax.all_gather(w_out, ("row", "col"), axis=0, tiled=True),
        lax.all_gather(w_gate_up, ("row", "col"), axis=0, tiled=True),
        lax.all_gather(w_down, ("row", "col"), axis=0, tiled=True),
        lax.all_gather(gain_attn, ("row", "col"), axis=0, tiled=True),
        lax.all_gather(gain_ffn, ("row", "col"), axis=0, tiled=True),
    )
    d_inner = contract_cols(cotangent, down_back)
    d_gate = (
        d_inner * upper_part * sigmoid_gate * (1.0 + gate_part * (1.0 - sigmoid_gate))
    ).astype(jnp.bfloat16)
    d_upper = (d_inner * active).astype(jnp.bfloat16)
    d_gate_up = jnp.concatenate([d_gate, d_upper], axis=1)
    d_scaled_two = contract_cols(d_gate_up, gate_up_back)
    term_gain_two = jnp.sum(d_scaled_two * normed_two, axis=0)
    term_gate_up = contract_rows(scaled_two, d_gate_up)
    term_down = contract_rows(inner_act, cotangent)
    d_hidden = cotangent.astype(jnp.float32) + norm_back(
        d_scaled_two * gain_two_back.astype(jnp.float32), normed_two, scale_two
    )
    d_branch = d_hidden.astype(jnp.bfloat16)
    term_out = contract_rows(attn_low, d_branch)
    d_attended = contract_cols(d_branch, out_back).reshape(tok_rows, head_count, HEAD_DIM)
    d_numerator = (d_attended / denominator.T[:, :, None]).astype(jnp.bfloat16)
    centre = (jnp.sum(d_attended * attended, axis=-1) / denominator.T).T
    back_keys = (
        lax.all_gather(key_own, "col", axis=0, tiled=True),
        lax.all_gather(value_own, "col", axis=0, tiled=True),
        lax.all_gather(seq_q, "col", axis=0, tiled=True),
        lax.all_gather(var_q, "col", axis=0, tiled=True),
    )

    def query_step(running, block_data):
        d_queries, same_sum, other_sum = running
        key_block, value_block, seq_block, var_block = block_data
        weights, matched = score_weights(
            queries, seq_q, var_q, key_block, seq_block, var_block, var_bias
        )
        d_probs = jnp.einsum(
            "qhd,khd->hqk", d_numerator, value_block, preferred_element_type=jnp.float32
        )
        d_scores = weights * (d_probs - centre[:, :, None])
        same_sum = same_sum + jnp.sum(jnp.where(matched[None], d_scores, 0.0), axis=(1, 2))
        other_sum = other_sum + jnp.sum(jnp.where(matched[None], 0.0, d_scores), axis=(1, 2))
        d_rounded = d_scores.astype(jnp.bfloat16)
        d_queries = d_queries + jnp.einsum(
            "hqk,khd->qhd", d_rounded, key_block, preferred_element_type=jnp.float32
        )
        return ((d_queries, same_sum, other_sum), (d_rounded, weights.astype(jnp.bfloat16)))

    def query_and_key_step(running, block_data):
        running, rounded = query_step(running, block_data)
        d_rounded, weights_low = rounded
        d_keys = (
            jnp.einsum("hqk,qhd->khd", d_rounded, queries, preferred_element_type=jnp.float32)
            * 0.125
        )
        d_values = jnp.einsum(
            "hqk,qhd->khd", weights_low, d_numerator, preferred_element_type=jnp.float32
        )
        return (running, (d_keys, d_values))

    start_running = (
        jnp.zeros((tok_rows, head_count, HEAD_DIM), jnp.float32),
        jnp.zeros((head_count,), jnp.float32),
        jnp.zeros((head_count,), jnp.float32),
    )
    (d_queries, same_sum, other_sum), (d_keys, d_values) = lax.scan(
        query_and_key_step,
        start_running,
        split_blocks(back_keys[0], back_keys[1], back_keys[2], back_keys[3]),
    )
    key_grad, value_grad = (
        lax.psum_scatter(
            d_keys.reshape(group_size, model_width).astype(jnp.bfloat16),
            "col",
            scatter_dimension=0,
            tiled=True,
        ).astype(jnp.float32),
        lax.psum_scatter(
            d_values.reshape(group_size, model_width).astype(jnp.bfloat16),
            "col",
            scatter_dimension=0,
            tiled=True,
        ).astype(jnp.float32),
    )
    d_query_pre = unrotate(d_queries * 0.125, cos_part, sin_part).reshape(tok_rows, model_width)
    d_key_pre = unrotate(
        key_grad.reshape(tok_rows, head_count, HEAD_DIM), cos_part, sin_part
    ).reshape(tok_rows, model_width)
    d_projected = jnp.concatenate([d_query_pre, d_key_pre, value_grad], axis=1).astype(jnp.bfloat16)
    d_scaled_one = contract_cols(d_projected, qkv_back)
    term_qkv = contract_rows(scaled_one, d_projected)
    term_gain_one = jnp.sum(d_scaled_one * normed_one, axis=0)
    grad_w_qkv, grad_w_out, grad_w_gate_up, grad_w_down, grad_gain_attn, grad_gain_ffn = (
        lax.psum_scatter(term_qkv, ("row", "col"), scatter_dimension=0, tiled=True),
        lax.psum_scatter(term_out, ("row", "col"), scatter_dimension=0, tiled=True),
        lax.psum_scatter(term_gate_up, ("row", "col"), scatter_dimension=0, tiled=True),
        lax.psum_scatter(term_down, ("row", "col"), scatter_dimension=0, tiled=True),
        lax.psum_scatter(term_gain_one, ("row", "col"), scatter_dimension=0, tiled=True),
        lax.psum_scatter(term_gain_two, ("row", "col"), scatter_dimension=0, tiled=True),
    )
    grad_var_bias = lax.psum(jnp.stack([same_sum, other_sum], axis=0), ("row", "col"))
    d_inputs = d_hidden + norm_back(
        d_scaled_one * gain_one_back.astype(jnp.float32), normed_one, scale_one
    )
    returned = lax.all_to_all(
        d_inputs.astype(jnp.bfloat16).reshape(n_col, piece_len, model_width),
        "col",
        split_axis=0,
        concat_axis=0,
        tiled=True,
    )
    grad_tokens = jnp.take(returned, target, axis=0).reshape(tok_rows, model_width)
    return (
        output,
        grad_tokens,
        grad_w_qkv,
        grad_w_out,
        grad_w_gate_up,
        grad_w_down,
        grad_gain_attn,
        grad_gain_ffn,
        grad_var_bias,
    )


def solution(mesh):
    return jax.shard_map(
        shards,
        mesh=mesh,
        in_specs=(
            P(("row", "col"), None),
            P(("row", "col")),
            P(("row", "col")),
            P("row", None),
            P("row", "col", None),
            P(("row", "col"), None),
            P(("row", "col"), None),
            P(("row", "col"), None),
            P(("row", "col"), None),
            P(("row", "col")),
            P(("row", "col")),
            P(),
            P(("row", "col"), None),
        ),
        out_specs=(
            P(("row", "col"), None),
            P(("row", "col"), None),
            P(("row", "col"), None),
            P(("row", "col"), None),
            P(("row", "col"), None),
            P(("row", "col"), None),
            P(("row", "col")),
            P(("row", "col")),
            P(),
        ),
        check_vma=False,
    )
```

profile of v0, /device:TPU:1, one launch (start us, length us, event | category | flops | bytes accessed | tf_op | source)
XLA Modules:
  0.0 1548.9 jit_solution(3545822266853017098)
XLA Ops:
  12.5 7.3 all-to-all-start.1
  21.3 4.6 all-to-all-done.1
  25.9 4.1 all-to-all-start
  31.7 41.9 %all-reduce.5 = (bf16[1024]{0:T(1024)(128)(2,1)S(1)}, bf16[1024]{0:T(1024)(128)(2,1)S(1)}) all-reduce(bf16[1024]{0:T(1024)(128)(2,1)S(1)} %dynamic-update-slice, bf16[1024]{0:T(1024)(128)(2,1)S(1)} %dynamic-update-slice.1), channel_id=1, replica_groups=mesh['row'=2,'col'=16] {'row','col'}, use_global_device_ids=true, to_apply=%add | all-reduce | flops 2048 | bytes 8192
  74.2 11.2 all-gather.9.cloned.1.call-done
  85.3 3.8 fusion.91
  89.2 1.6 copy.80
  90.8 1.3 slice_bitcast_fusion.4
  96.3 19.8 %all-gather = s32[16,1,128]{2,1,0:T(1,128)S(1)} all-gather(s32[1,1,128]{2,1,0:T(1,128)S(1)} %reshape.400), channel_id=1, replica_groups=mesh['row'=2,'col'=16] {'col'}, dimensions={0}, use_global_device_ids=true | all-gather | bytes 8704 | tf_op jit(solution)/shard_map/all_gather | solution.py:137
  117.4 17.5 %all-gather.1 = s32[16,1,128]{2,1,0:T(1,128)S(1)} all-gather(s32[1,1,128]{2,1,0:T(1,128)S(1)} %reshape.402), channel_id=1, replica_groups=mesh['row'=2,'col'=16] {'col'}, dimensions={0}, use_global_device_ids=true | all-gather | bytes 8704 | tf_op jit(solution)/shard_map/all_gather | solution.py:138
  135.7 9.3 all-gather.11.cloned.1.call-done
  145.0 7.9 reshape.357
  152.8 5.7 copy.83
  158.5 38.1 %all-gather.13.cloned.1.call-done = bf16[2048,1024]{1,0:T(8,128)(2,1)} async-done(((bf16[128,1024]{1,0:T(8,128)(2,1)}), bf16[2048,1024]{1,0:T(8,128)(2,1)}) %all-gather.13.cloned.1.call-update) | async-done | bytes 4194320 | tf_op jit(solution)/shard_map/all_gather | solution.py:136
  196.7 11.6 reshape.416
  208.3 9.8 copy.85
  218.1 31.7 %while.34 = (s32[]{:T(128)}, f32[16,128]{1,0:T(8,128)S(1)}, f32[128,16,64]{0,2,1:T(8,128)S(1)}, s32[16,1,8]{2,0,1:T(8,128)}, s32[2,1024]{1,0:T(2,128)S(1)}, /*in...) while((s32[]{:T(128)}, f32[16,128]{1,0:T(8,128)S(1)}, ...), condition=%wide.wide.region_6.8_spmd.clone, body=%wide.wide.region_4.7_spmd.clone.sunk | while | flops 558368768 | bytes 23127724 | solution.py:165
  218.5 8.7 fusion.161
  227.2 6.6 fusion.162
  234.2 8.7 fusion.161
  242.9 6.6 fusion.162
  249.8 4.5 all-gather.15.cloned.1.call-done
  254.3 2.1 multiply_reduce_fusion.3
  256.5 114.3 %all-gather.17.cloned.1.call-done = bf16[1024,8192]{1,0:T(8,128)(2,1)} async-done(((bf16[32,8192]{1,0:T(8,128)(2,1)}), bf16[1024,8192]{1,0:T(8,128)(2,1)}) %all-gather.17.cloned.1.call-update) | async-done | bytes 16777232 | tf_op jit(solution)/shard_map/all_gather | solution.py:119
  370.8 10.2 fusion.99
  381.0 68.3 %all-gather.19.cloned.1.call-done = bf16[4096,1024]{1,0:T(8,128)(2,1)} async-done(((bf16[128,1024]{1,0:T(8,128)(2,1)}), bf16[4096,1024]{1,0:T(8,128)(2,1)}) %all-gather.19.cloned.1.call-update) | async-done | bytes 8388624 | tf_op jit(solution)/shard_map/all_gather | solution.py:120
  449.3 9.1 multiply_convert_fusion.1
  458.5 13.5 multiply_reduce_fusion
  472.0 1.3 multiply_add_fusion
  473.3 2.3 fusion.88
  476.4 46.5 %while.35 = (s32[]{:T(128)}, f32[128,16,64]{0,2,1:T(8,128)S(1)}, f32[16]{0:T(128)S(1)}, f32[16]{0:T(128)S(1)}, bf16[2,1024,16,64]{1,3,2,0:T(8,128)(2,1)}, /*inde...) while((s32[]{:T(128)}, f32[128,16,64]{0,2,1:T(8,128)S(1)}, ...), condition=%wide.wide.region_13.15_spmd.clone, body=%wide.wide.region_10.14_spmd.clone.sunk | while | flops 1377304576 | bytes 158108944 | solution.py:256
  477.1 3.1 fusion.172
  480.4 7.2 select_reduce_fusion.5
  487.7 3.9 fusion.173
  491.7 2.9 bitcast_dynamic-update-slice_fusion.6
  494.6 1.2 copy-done.4
  495.8 4.1 bitcast_dynamic-update-slice_fusion.7
  500.1 3.1 fusion.172
  503.5 7.2 select_reduce_fusion.5
  510.7 3.9 fusion.173
  514.7 3.0 bitcast_dynamic-update-slice_fusion.6
  517.7 1.2 copy-done.4
  518.9 4.1 bitcast_dynamic-update-slice_fusion.7
  523.0 10.9 copy.104
  533.9 11.9 reshape.412
  545.8 11.2 copy.105
  557.0 12.0 reshape.414
  570.0 2.8 fusion.86
  573.8 41.2 %reduce-scatter.19.cloned.1.call-done = bf16[128,1024]{1,0:T(8,128)(2,1)} async-done(((bf16[2048,1024]{1,0:T(8,128)(2,1)}), bf16[128,1024]{1,0:T(8,128)(2,1)}) %reduce-scatter.19.cloned.1.call-update) | async-done | bytes 262160
  614.9 1.1 copy.99
  616.1 74.7 %reduce-scatter.21.cloned.1.call-done = bf16[128,1024]{1,0:T(8,128)(2,1)} async-done(((bf16[2048,1024]{1,0:T(8,128)(2,1)}), bf16[128,1024]{1,0:T(8,128)(2,1)}) %reduce-scatter.21.cloned.1.call-update) | async-done | bytes 262160
  690.8 1.1 copy.101
  691.9 1.2 add_convert_fusion.1
  693.2 6.4 fusion.82
  700.6 8.1 fusion.100
  708.7 14.9 fusion.66
  724.3 5.1 fusion.80
  730.3 6.0 all-to-all-start.2
  736.3 5.4 fusion.68
  741.7 40.7 %all-reduce.4 = (f32[1024]{0:T(1024)S(1)}, f32[1024]{0:T(1024)S(1)}, f32[2,16]{1,0:T(2,128)}) all-reduce(f32[1024]{0:T(1024)S(1)} %get-tuple-element.360, f32[1024]{0:T(1024)S(1)} %copy-done.25, f32[2,16]{1,0:T(2,128)S(1)} %pad_maximum_fusion.10), channel_id=8, replica_groups=mesh['row'=2,'col'=16] {'row','col'}, use_global_device_ids=true, to_apply=%region_22.24.clone | all-reduce | flops 2080 | bytes 16640
  784.9 45.3 %reduce-scatter.13.cloned.1.call-done = f32[32,1024]{1,0:T(8,128)} async-done(((f32[1024,1024]{1,0:T(8,128)}), f32[32,1024]{1,0:T(8,128)}) %reduce-scatter.13.cloned.1.call-update) | async-done | bytes 131088 | tf_op jit(solution)/shard_map/reduce_scatter | solution.py:285
  830.2 162.6 %reduce-scatter.11.cloned.1.call-done = f32[32,3072]{1,0:T(8,128)} async-done(((f32[1024,3072]{1,0:T(8,128)}), f32[32,3072]{1,0:T(8,128)}) %reduce-scatter.11.cloned.1.call-update) | async-done | bytes 393232 | tf_op jit(solution)/shard_map/reduce_scatter | solution.py:284
  992.8 187.5 %reduce-scatter.17.cloned.1.call-done = f32[128,1024]{1,0:T(8,128)} async-done(((f32[4096,1024]{1,0:T(8,128)}), f32[128,1024]{1,0:T(8,128)}) %reduce-scatter.17.cloned.1.call-update) | async-done | bytes 524304 | tf_op jit(solution)/shard_map/reduce_scatter | solution.py:287
  1180.3 361.5 %reduce-scatter.15.cloned.1.call-done = f32[32,8192]{1,0:T(8,128)} async-done(((f32[1024,8192]{1,0:T(8,128)}), f32[32,8192]{1,0:T(8,128)}) %reduce-scatter.15.cloned.1.call-update) | async-done | bytes 1048592 | tf_op jit(solution)/shard_map/reduce_scatter | solution.py:286
  (184 shorter events, 24.9 us)
Async XLA Ops:
  7.2 12.7 copy-start
  7.2 78.1 %all-gather.9.cloned.1.call-start = ((), (), s32[]{:S(2)}) async-start(), calls=%async_computation.9 | async-start | bytes 6488064 | tf_op jit(solution)/shard_map/all_gather | solution.py:117
  12.5 13.4 all-to-all-start.1
  25.9 48.0 %all-to-all-start = ((bf16[16,8,1024]{2,1,0:T(8,128)(2,1)}), bf16[16,8,1024]{2,1,0:T(8,128)(2,1)S(1)}, u32[]{:S(2)}, u32[]{:S(2)}) async-start(bf16[16,8,1024]{2,1,0:T(8,128)(2,1)} %broadcast_select_fusion.2), calls=%async_computation | async-start | bytes 524288 | tf_op jit(solution)/shard_map/all_to_all | solution.py:109
  29.9 115.0 %all-gather.11.cloned.1.call-start = ((), (), s32[]{:S(2)}) async-start(), calls=%async_computation.10 | async-start | bytes 4456448 | tf_op jit(solution)/shard_map/all_gather | solution.py:135
  73.6 15.6 %copy-start.12 = (f32[1024]{0:T(1024)}, f32[1024]{0:T(1024)S(1)}, u32[]{:S(2)}) copy-start(f32[1024]{0:T(1024)S(1)} %convert_element_type.102) | copy-start | bytes 12292
  73.9 18.2 %copy-start.16 = (f32[128,32]{0,1:T(8,128)}, f32[128,32]{0,1:T(8,128)S(1)}, u32[]{:S(2)}) copy-start(f32[128,32]{0,1:T(8,128)S(1)} %get-tuple-element.455) | copy-start | bytes 49156
  73.9 18.2 %copy-start.18 = (f32[128,32]{0,1:T(8,128)}, f32[128,32]{0,1:T(8,128)S(1)}, u32[]{:S(2)}) copy-start(f32[128,32]{0,1:T(8,128)S(1)} %get-tuple-element.456) | copy-start | bytes 49156
  74.2 15.0 copy-start.23
  93.1 103.6 %all-gather.13.cloned.1.call-start = ((), (), s32[]{:S(2)}) async-start(), calls=%async_computation.11 | async-start | bytes 4456448 | tf_op jit(solution)/shard_map/all_gather | solution.py:136
  93.9 160.5 %all-gather.15.cloned.1.call-start = ((), (), s32[]{:S(2)}) async-start(), calls=%async_computation.12 | async-start | bytes 2162688 | tf_op jit(solution)/shard_map/all_gather | solution.py:118
  94.5 276.4 %all-gather.17.cloned.1.call-start = ((), (), s32[]{:S(2)}) async-start(), calls=%async_computation.13 | async-start | bytes 17301504 | tf_op jit(solution)/shard_map/all_gather | solution.py:119
  95.0 354.3 %all-gather.19.cloned.1.call-start = ((), (), s32[]{:S(2)}) async-start(), calls=%async_computation.14 | async-start | bytes 8650752 | tf_op jit(solution)/shard_map/all_gather | solution.py:120
  95.6 519.3 %reduce-scatter.19.cloned.1.call-start = ((), (), s32[]{:S(2)}) async-start(), calls=%async_computation.19 | async-start | bytes 4456448
  95.8 57.0 %copy-start.21 = (s32[16,1,8]{2,1,0:T(1,128)}, s32[16,1,8]{2,1,0:T(1,128)S(1)}, u32[]{:S(2)}) copy-start(s32[16,1,8]{2,1,0:T(1,128)S(1)} %get-tuple-element.449) | copy-start | bytes 1540
  95.8 57.0 %copy-start.22 = (s32[16,1,8]{2,1,0:T(1,128)}, s32[16,1,8]{2,1,0:T(1,128)S(1)}, u32[]{:S(2)}) copy-start(s32[16,1,8]{2,1,0:T(1,128)S(1)} %get-tuple-element.452) | copy-start | bytes 1540
  208.3 9.8 copy-start.20
  249.7 131.2 %copy-start.8 = (f32[128,16,64]{0,2,1:T(8,128)}, f32[128,16,64]{0,2,1:T(8,128)S(1)}, u32[]{:S(2)}) copy-start(f32[128,16,64]{0,2,1:T(8,128)S(1)} %get-tuple-element.154) | copy-start | bytes 1572868
  249.8 131.2 %copy-start.6 = (bf16[128,16,64]{0,2,1:T(8,128)(2,1)}, bf16[128,16,64]{0,2,1:T(8,128)(2,1)S(1)}, u32[]{:S(2)}) copy-start(bf16[128,16,64]{0,2,1:T(8,128)(2,1)S(1)} %fusion.85) | copy-start | bytes 786436
  370.8 78.5 %copy-start.10 = (bf16[128,1024]{1,0:T(8,128)(2,1)S(1)}, bf16[128,1024]{1,0:T(8,128)(2,1)}, u32[]{:S(2)}) copy-start(bf16[128,1024]{1,0:T(8,128)(2,1)} %param.31) | copy-start | bytes 786436
  472.0 3.6 copy-start.9
  477.1 3.4 copy-start.5
  477.1 3.4 copy-start.14
  480.2 7.5 copy-start.3
  487.7 4.0 copy-start.2
  491.7 4.1 copy-start.4
  491.7 4.1 copy-start.15
  500.1 3.4 copy-start.5
  500.1 3.4 copy-start.14
  503.3 7.5 copy-start.3
  510.7 4.0 copy-start.2
  514.7 4.1 copy-start.4
  514.7 4.1 copy-start.15
  545.8 145.0 %reduce-scatter.21.cloned.1.call-start = ((), (), s32[]{:S(2)}) async-start(), calls=%async_computation.20 | async-start | bytes 4456448
  569.1 0.9 copy-start.7
  569.1 261.1 %reduce-scatter.13.cloned.1.call-start = ((), (), s32[]{:S(2)}) async-start(), calls=%async_computation.16 | async-start | bytes 4325376 | tf_op jit(solution)/shard_map/reduce_scatter | solution.py:285
  572.8 119.1 %copy-start.17 = (f32[128,32]{0,1:T(8,128)S(1)}, f32[128,32]{0,1:T(8,128)}, u32[]{:S(2)}) copy-start(f32[128,32]{0,1:T(8,128)} %copy-done.16) | copy-start | bytes 49156
  572.8 119.1 %copy-start.19 = (f32[128,32]{0,1:T(8,128)S(1)}, f32[128,32]{0,1:T(8,128)}, u32[]{:S(2)}) copy-start(f32[128,32]{0,1:T(8,128)} %copy-done.18) | copy-start | bytes 49156
  572.9 120.3 %copy-start.13 = (f32[1024]{0:T(1024)S(1)}, f32[1024]{0:T(1024)}, u32[]{:S(2)}) copy-start(f32[1024]{0:T(1024)} %copy-done.12) | copy-start | bytes 12292
  572.9 120.4 %copy-start.24 = (f32[128]{0:T(128)S(1)}, f32[128]{0:T(128)}, u32[]{:S(2)}) copy-start(f32[128]{0:T(128)} %copy-done.23) | copy-start | bytes 1540
  572.9 419.9 %reduce-scatter.11.cloned.1.call-start = ((), (), s32[]{:S(2)}) async-start(), calls=%async_computation.15 | async-start | bytes 12976128 | tf_op jit(solution)/shard_map/reduce_scatter | solution.py:284
  699.6 1.0 copy-start.11
  699.6 480.7 %reduce-scatter.17.cloned.1.call-start = ((), (), s32[]{:S(2)}) async-start(), calls=%async_computation.18 | async-start | bytes 17301504 | tf_op jit(solution)/shard_map/reduce_scatter | solution.py:287
  708.7 833.2 %reduce-scatter.15.cloned.1.call-start = ((), (), s32[]{:S(2)}) async-start(), calls=%async_computation.17 | async-start | bytes 34603008 | tf_op jit(solution)/shard_map/reduce_scatter | solution.py:286
  723.6 0.7 copy-start.26
  730.3 53.2 %all-to-all-start.2 = ((bf16[16,8,1024]{2,1,0:T(8,128)(2,1)}), bf16[16,8,1024]{2,1,0:T(8,128)(2,1)S(1)}, u32[]{:S(2)}, u32[]{:S(2)}) async-start(bf16[16,8,1024]{2,1,0:T(8,128)(2,1)} %fusion.84), calls=%async_computation.2 | async-start | bytes 524288 | tf_op jit(solution)/shard_map/all_to_all | solution.py:295
  736.3 5.4 copy-start.25
  736.3 805.5 %copy-start.1 = (bf16[128,1024]{1,0:T(8,128)(2,1)S(1)}, bf16[128,1024]{1,0:T(8,128)(2,1)}, u32[]{:S(2)}) copy-start(bf16[128,1024]{1,0:T(8,128)(2,1)} %param.19) | copy-start | bytes 786436
Sparse Core Ops, SparseCore 0:
  10.9 74.3 all-gather.8
  93.2 51.7 all-gather.10
  147.7 48.8 all-gather.12
  199.4 54.9 all-gather.14
  257.1 113.7 all-gather.16
  373.6 75.7 all-gather.18
  545.9 68.9 reduce-scatter.18
  619.3 71.4 reduce-scatter.20
  693.7 136.5 reduce-scatter.12
  836.7 156.0 reduce-scatter.10
  995.8 184.4 reduce-scatter.16
  1183.1 358.6 reduce-scatter.14
where the time goes:
time: 1560 us; the launch traced here: 1550 us
  waiting for transfers between devices  1130 us (72%)
  matrix products  157 us (10%)
  blocking collectives  120 us (8%)
  local copies, waits for them, and re-layouts  99.4 us (6%)
  starting transfers between devices  17.8 us (1%)
    reduce_scatter x1, waiting for transfers between devices, shards(): lax.psum_scatter(term_gate_up, ('row', 'col'), scatter_dimension=0, tiled...  362 us
    reduce_scatter x1, waiting for transfers between devices, shards(): lax.psum_scatter(term_down, ('row', 'col'), scatter_dimension=0, tiled=True)  187 us
    reduce_scatter x1, waiting for transfers between devices, shards(): lax.psum_scatter(term_qkv, ('row', 'col'), scatter_dimension=0, tiled=True)  163 us
    unnamed x14, waiting for transfers between devices  118 us
    all_gather x1, waiting for transfers between devices, shards(): lax.all_gather(w_gate_up, ('row', 'col'), axis=0, tiled=True)  114 us
    unnamed x2, blocking collectives  82.6 us
    unnamed x58, local copies, waits for them, and re-layouts  69.2 us
    all_gather x1, waiting for transfers between devices, shards(): lax.all_gather(w_down, ('row', 'col'), axis=0, tiled=True)  68.3 us
  transfers between devices with their start and end apart: 15, of which 13 were waited for; matrix products, arithmetic and copies ran while one was open for 11% of the time, Pallas kernels for 0%

commit v1 on v0

--- a/solution.py
+++ b/solution.py
@@ -8,6 +8,22 @@
 UNIT = 128
 KEY_BLOCK = 1024
 epsilon = 1e-05
+
+
+def collect(x, axis, dim):
+    ways, here, step = (lax.axis_size(axis), lax.axis_index(axis), x.shape[dim])
+    shape = [n * ways if d == dim else n for d, n in enumerate(x.shape)]
+    full = lax.dynamic_update_slice_in_dim(jnp.zeros(shape, x.dtype), x, here * step, axis=dim)
+    going_up = going_down = x
+    for far in range(1, ways // 2 + 1):
+        going_up = lax.ppermute(going_up, axis, [(d, (d + 1) % ways) for d in range(ways)])
+        full = lax.dynamic_update_slice_in_dim(full, going_up, (here - far) % ways * step, axis=dim)
+        if 2 * far < ways:
+            going_down = lax.ppermute(going_down, axis, [(d, (d - 1) % ways) for d in range(ways)])
+            full = lax.dynamic_update_slice_in_dim(
+                full, going_down, (here + far) % ways * step, axis=dim
+            )
+    return full
 
 
 def contract_rows(operand, factor):
@@ -133,7 +149,7 @@
     value_own = projected[:, 2 * model_width :].astype(jnp.bfloat16)
     keys_all, values_all, seq_k, var_k = (
         lax.all_gather(key_own, "col", axis=0, tiled=True),
-        lax.all_gather(value_own, "col", axis=0, tiled=True),
+        collect(value_own, "col", 0),
         lax.all_gather(seq_q, "col", axis=0, tiled=True),
         lax.all_gather(var_q, "col", axis=0, tiled=True),
     )

time: 1560 us -> 1580 us (1.013)
  waiting for transfers between devices: 1130 us -> 1080 us
  local copies, waits for them, and re-layouts: 99.4 us -> 132 us
  starting transfers between devices: 17.8 us -> 47.3 us
    all_gather x1, waiting for transfers between devices: 38.1 us -> 0.01 us  [shards(): lax.all_gather(value_own, 'col', axis=0, tiled=True)]
    ppermute x0 -> x15, starting transfers between devices: none -> 30.1 us  [the longest x7 15.3 us: collect(): lax.ppermute(going_down, axis, [(d, (d - 1) % ways) for d in range(ways)])]
    ppermute x0 -> x15, waiting for transfers between devices: none -> 22.2 us  [the longest x7 12 us: collect(): lax.ppermute(going_down, axis, [(d, (d - 1) % ways) for d in range(ways)])]
    all_gather x1, waiting for transfers between devices: 114 us -> 97.5 us  [shards(): lax.all_gather(w_gate_up, ('row', 'col'), axis=0, tiled=True)]
    unnamed x58 -> x59, local copies, waits for them, and re-layouts: 69.2 us -> 74.7 us
  transfers between devices with their start and end apart: 15 -> 30, of which waited for: 13 -> 18; matrix products, arithmetic and copies ran while one was open for 11% -> 13% of each run, Pallas kernels for 0% -> 0%
where the time goes in v1:
time: 1580 us; the launch traced here: 1570 us
  waiting for transfers between devices  1080 us (68%)
  matrix products  157 us (10%)
  local copies, waits for them, and re-layouts  132 us (8%)
  blocking collectives  124 us (8%)
  starting transfers between devices  47.3 us (3%)
    reduce_scatter x1, waiting for transfers between devices, shards(): lax.psum_scatter(term_gate_up, ('row', 'col'), scatter_dimension=0, tiled...  362 us
    reduce_scatter x1, waiting for transfers between devices, shards(): lax.psum_scatter(term_down, ('row', 'col'), scatter_dimension=0, tiled=True)  187 us
    reduce_scatter x1, waiting for transfers between devices, shards(): lax.psum_scatter(term_qkv, ('row', 'col'), scatter_dimension=0, tiled=True)  163 us
    unnamed x14, waiting for transfers between devices  119 us
    all_gather x1, waiting for transfers between devices, shards(): lax.all_gather(w_gate_up, ('row', 'col'), axis=0, tiled=True)  97.5 us
    unnamed x2, blocking collectives  83 us
    unnamed x59, local copies, waits for them, and re-layouts  74.7 us
    all_gather x1, waiting for transfers between devices, shards(): lax.all_gather(w_down, ('row', 'col'), axis=0, tiled=True)  68.3 us
  transfers between devices with their start and end apart: 30, of which 18 were waited for; matrix products, arithmetic and copies ran while one was open for 13% of the time, Pallas kernels for 0%

profile of v1, /device:TPU:1, one launch (start us, length us, event | category | flops | bytes accessed | tf_op | source)
XLA Modules:
  0.0 1569.8 jit_solution(5466802563144078026)
XLA Ops:
  12.5 7.3 all-to-all-start.1
  21.3 4.6 all-to-all-done.1
  25.9 4.1 all-to-all-start
  31.7 41.9 %all-reduce.5 = (bf16[1024]{0:T(1024)(128)(2,1)S(1)}, bf16[1024]{0:T(1024)(128)(2,1)S(1)}) all-reduce(bf16[1024]{0:T(1024)(128)(2,1)S(1)} %dynamic-update-slice, bf16[1024]{0:T(1024)(128)(2,1)S(1)} %dynamic-update-slice.1), channel_id=1, replica_groups=mesh['row'=2,'col'=16] {'row','col'}, use_global_device_ids=true, to_apply=%add | all-reduce | flops 2048 | bytes 8192
  74.2 11.2 all-gather.9.cloned.1.call-done
  85.3 3.8 fusion.91
  97.1 5.4 collective-permute-done
  102.4 2.9 collective-permute-start.2
  105.3 3.5 collective-permute-done.1
  109.0 2.5 collective-permute-start.4
  111.5 4.6 collective-permute-done.3
  116.6 24.2 %all-gather = s32[16,1,128]{2,1,0:T(1,128)S(1)} all-gather(s32[1,1,128]{2,1,0:T(1,128)S(1)} %reshape.403), channel_id=1, replica_groups=mesh['row'=2,'col'=16] {'col'}, dimensions={0}, use_global_device_ids=true | all-gather | bytes 8704 | tf_op jit(solution)/shard_map/all_gather | solution.py:153
  142.1 17.3 %all-gather.1 = s32[16,1,128]{2,1,0:T(1,128)S(1)} all-gather(s32[1,1,128]{2,1,0:T(1,128)S(1)} %reshape.405), channel_id=1, replica_groups=mesh['row'=2,'col'=16] {'col'}, dimensions={0}, use_global_device_ids=true | all-gather | bytes 8704 | tf_op jit(solution)/shard_map/all_gather | solution.py:154
  162.8 2.5 broadcast_in_dim.143
  170.9 3.2 collective-permute-done.7
  180.0 7.8 collective-permute-start.11
  193.4 5.3 collective-permute-start.13
  200.6 4.1 collective-permute-done.12
  204.7 2.6 collective-permute-start.14
  211.5 7.9 reshape.361
  219.4 5.5 copy.131
  224.9 7.9 reshape.359
  232.8 5.5 copy.129
  238.3 11.6 reshape.415
  249.9 9.8 copy.137
  259.7 32.2 %while.34 = (s32[]{:T(128)}, f32[16,128]{1,0:T(8,128)S(1)}, f32[128,16,64]{0,2,1:T(8,128)S(1)}, s32[16,1,8]{2,0,1:T(8,128)}, s32[2,1024]{1,0:T(2,128)S(1)}, /*in...) while((s32[]{:T(128)}, f32[16,128]{1,0:T(8,128)S(1)}, ...), condition=%wide.wide.region_6.8_spmd.clone, body=%wide.wide.region_4.7_spmd.clone.sunk | while | flops 558368768 | bytes 23127724 | solution.py:181
  260.2 8.7 fusion.161
  268.9 6.7 fusion.162
  276.1 8.7 fusion.161
  284.8 6.9 fusion.162
  294.3 97.5 %all-gather.15.cloned.1.call-done = bf16[1024,8192]{1,0:T(8,128)(2,1)} async-done(((bf16[32,8192]{1,0:T(8,128)(2,1)}), bf16[1024,8192]{1,0:T(8,128)(2,1)}) %all-gather.15.cloned.1.call-update) | async-done | bytes 16777232 | tf_op jit(solution)/shard_map/all_gather | solution.py:135
  391.8 10.2 fusion.99
  402.0 68.3 %all-gather.17.cloned.1.call-done = bf16[4096,1024]{1,0:T(8,128)(2,1)} async-done(((bf16[128,1024]{1,0:T(8,128)(2,1)}), bf16[4096,1024]{1,0:T(8,128)(2,1)}) %all-gather.17.cloned.1.call-update) | async-done | bytes 8388624 | tf_op jit(solution)/shard_map/all_gather | solution.py:136
  470.3 9.1 multiply_convert_fusion.1
  479.5 13.5 multiply_reduce_fusion
  497.4 46.6 %while.35 = (s32[]{:T(128)}, f32[128,16,64]{0,2,1:T(8,128)S(1)}, f32[16]{0:T(128)S(1)}, f32[16]{0:T(128)S(1)}, bf16[2,1024,16,64]{1,3,2,0:T(8,128)(2,1)}, /*inde...) while((s32[]{:T(128)}, f32[128,16,64]{0,2,1:T(8,128)S(1)}, ...), condition=%wide.wide.region_13.15_spmd.clone, body=%wide.wide.region_10.14_spmd.clone.sunk | while | flops 1377304576 | bytes 158108944 | solution.py:272
  498.1 3.1 fusion.172
  501.5 7.2 select_reduce_fusion.5
  508.7 3.9 fusion.173
  512.7 3.0 bitcast_dynamic-update-slice_fusion.6
  516.9 4.1 bitcast_dynamic-update-slice_fusion.7
  521.2 3.1 fusion.172
  524.5 7.2 select_reduce_fusion.5
  531.8 3.9 fusion.173
  535.8 2.9 bitcast_dynamic-update-slice_fusion.6
  539.9 4.1 bitcast_dynamic-update-slice_fusion.7
  544.0 11.0 copy.151
  555.0 11.9 reshape.416
  567.0 11.2 copy.152
  578.2 12.0 reshape.418
  591.2 2.8 fusion.86
  595.0 41.7 %reduce-scatter.19.cloned.1.call-done = bf16[128,1024]{1,0:T(8,128)(2,1)} async-done(((bf16[2048,1024]{1,0:T(8,128)(2,1)}), bf16[128,1024]{1,0:T(8,128)(2,1)}) %reduce-scatter.19.cloned.1.call-update) | async-done | bytes 262160
  637.8 74.6 %reduce-scatter.21.cloned.1.call-done = bf16[128,1024]{1,0:T(8,128)(2,1)} async-done(((bf16[2048,1024]{1,0:T(8,128)(2,1)}), bf16[128,1024]{1,0:T(8,128)(2,1)}) %reduce-scatter.21.cloned.1.call-update) | async-done | bytes 262160
  714.9 6.4 fusion.82
  722.2 8.1 fusion.100
  730.4 14.9 fusion.66
  746.0 5.1 fusion.80
  752.1 5.4 all-to-all-start.2
  757.4 5.4 fusion.68
  762.8 41.1 %all-reduce.4 = (f32[1024]{0:T(1024)S(1)}, f32[1024]{0:T(1024)S(1)}, f32[2,16]{1,0:T(2,128)}) all-reduce(f32[1024]{0:T(1024)S(1)} %get-tuple-element.349, f32[1024]{0:T(1024)S(1)} %copy-done.25, f32[2,16]{1,0:T(2,128)S(1)} %pad_maximum_fusion.10), channel_id=8, replica_groups=mesh['row'=2,'col'=16] {'row','col'}, use_global_device_ids=true, to_apply=%region_22.24.clone | all-reduce | flops 2080 | bytes 16640
  806.4 44.9 %reduce-scatter.13.cloned.1.call-done = f32[32,1024]{1,0:T(8,128)} async-done(((f32[1024,1024]{1,0:T(8,128)}), f32[32,1024]{1,0:T(8,128)}) %reduce-scatter.13.cloned.1.call-update) | async-done | bytes 131088 | tf_op jit(solution)/shard_map/reduce_scatter | solution.py:301
  851.4 162.5 %reduce-scatter.11.cloned.1.call-done = f32[32,3072]{1,0:T(8,128)} async-done(((f32[1024,3072]{1,0:T(8,128)}), f32[32,3072]{1,0:T(8,128)}) %reduce-scatter.11.cloned.1.call-update) | async-done | bytes 393232 | tf_op jit(solution)/shard_map/reduce_scatter | solution.py:300
  1013.9 187.4 %reduce-scatter.17.cloned.1.call-done = f32[128,1024]{1,0:T(8,128)} async-done(((f32[4096,1024]{1,0:T(8,128)}), f32[128,1024]{1,0:T(8,128)}) %reduce-scatter.17.cloned.1.call-update) | async-done | bytes 524304 | tf_op jit(solution)/shard_map/reduce_scatter | solution.py:303
  1201.2 361.5 %reduce-scatter.15.cloned.1.call-done = f32[32,8192]{1,0:T(8,128)} async-done(((f32[1024,8192]{1,0:T(8,128)}), f32[32,8192]{1,0:T(8,128)}) %reduce-scatter.15.cloned.1.call-update) | async-done | bytes 1048592 | tf_op jit(solution)/shard_map/reduce_scatter | solution.py:302
  (249 shorter events, 66.7 us)
Async XLA Ops:
  7.2 12.7 copy-start
  7.2 78.1 %all-gather.9.cloned.1.call-start = ((), (), s32[]{:S(2)}) async-start(), calls=%async_computation.9 | async-start | bytes 6488064 | tf_op jit(solution)/shard_map/all_gather | solution.py:133
  12.5 13.4 all-to-all-start.1
  25.9 48.0 %all-to-all-start = ((bf16[16,8,1024]{2,1,0:T(8,128)(2,1)}), bf16[16,8,1024]{2,1,0:T(8,128)(2,1)S(1)}, u32[]{:S(2)}, u32[]{:S(2)}) async-start(bf16[16,8,1024]{2,1,0:T(8,128)(2,1)} %broadcast_select_fusion.2), calls=%async_computation | async-start | bytes 524288 | tf_op jit(solution)/shard_map/all_to_all | solution.py:125
  29.9 195.0 %all-gather.11.cloned.1.call-start = ((), (), s32[]{:S(2)}) async-start(), calls=%async_computation.10 | async-start | bytes 4456448 | tf_op jit(solution)/shard_map/all_gather | solution.py:151
  73.6 15.6 copy-start.12
  73.9 18.3 %copy-start.16 = (f32[128,32]{0,1:T(8,128)}, f32[128,32]{0,1:T(8,128)S(1)}, u32[]{:S(2)}) copy-start(f32[128,32]{0,1:T(8,128)S(1)} %get-tuple-element.444) | copy-start | bytes 49156
  73.9 18.3 %copy-start.18 = (f32[128,32]{0,1:T(8,128)}, f32[128,32]{0,1:T(8,128)S(1)}, u32[]{:S(2)}) copy-start(f32[128,32]{0,1:T(8,128)S(1)} %get-tuple-element.445) | copy-start | bytes 49156
  74.2 15.0 copy-start.23
  93.1 145.2 %all-gather.19.cloned.1.call-start = ((), (), s32[]{:S(2)}) async-start(), calls=%async_computation.14 | async-start | bytes 4456448 | tf_op jit(solution)/shard_map/all_gather | solution.py:232
  93.9 198.1 %all-gather.13.cloned.1.call-start = ((), (), s32[]{:S(2)}) async-start(), calls=%async_computation.11 | async-start | bytes 2162688 | tf_op jit(solution)/shard_map/all_gather | solution.py:134
  94.5 297.3 %all-gather.15.cloned.1.call-start = ((), (), s32[]{:S(2)}) async-start(), calls=%async_computation.12 | async-start | bytes 17301504 | tf_op jit(solution)/shard_map/all_gather | solution.py:135
  95.1 375.3 %all-gather.17.cloned.1.call-start = ((), (), s32[]{:S(2)}) async-start(), calls=%async_computation.13 | async-start | bytes 8650752 | tf_op jit(solution)/shard_map/all_gather | solution.py:136
  95.6 541.0 %reduce-scatter.19.cloned.1.call-start = ((), (), s32[]{:S(2)}) async-start(), calls=%async_computation.19 | async-start | bytes 4456448
  95.7 6.8 collective-permute-start
  97.1 11.8 collective-permute-start.1
  102.4 6.6 collective-permute-start.2
  108.8 7.2 collective-permute-start.3
  109.0 52.2 %collective-permute-start.4 = (bf16[128,1024]{1,0:T(8,128)(2,1)S(1)}, bf16[128,1024]{1,0:T(8,128)(2,1)S(1)}, u32[]{:S(2)}, u32[]{:S(2)}) collective-permute-start(bf16[128,1024]{1,0:T(8,128)(2,1)S(1)} %collective-permute-done.2), channel_id=1, source_target_pairs={{0,1},{1,2},{2,3},{3,4},{4,5},{5,6},{6,7},{7,8},{8,9},{9,10},{10,1... | collective-permute-start | bytes 786440 | tf_op jit(solution)/shard_map/ppermute | solution.py:19
  116.1 50.2 %collective-permute-start.5 = (bf16[128,1024]{1,0:T(8,128)(2,1)S(1)}, bf16[128,1024]{1,0:T(8,128)(2,1)}, u32[]{:S(2)}, u32[]{:S(2)}) collective-permute-start(bf16[128,1024]{1,0:T(8,128)(2,1)S(1)} %collective-permute-done.3), channel_id=1, source_target_pairs={{0,15},{1,0},{2,1},{3,2},{4,3},{5,4},{6,5},{7,6},{8,7},{9,8},{10,9... | collective-permute-start | bytes 786440 | tf_op jit(solution)/shard_map/ppermute | solution.py:22
  116.1 52.1 %copy-start.21 = (s32[16,1,8]{2,1,0:T(1,128)}, s32[16,1,8]{2,1,0:T(1,128)S(1)}, u32[]{:S(2)}) copy-start(s32[16,1,8]{2,1,0:T(1,128)S(1)} %get-tuple-element.438) | copy-start | bytes 1540
  116.1 52.1 %copy-start.22 = (s32[16,1,8]{2,1,0:T(1,128)}, s32[16,1,8]{2,1,0:T(1,128)S(1)}, u32[]{:S(2)}) copy-start(s32[16,1,8]{2,1,0:T(1,128)S(1)} %get-tuple-element.441) | copy-start | bytes 1540
  161.3 7.0 collective-permute-start.6
  166.3 7.9 collective-permute-start.7
  168.2 10.9 collective-permute-start.8
  174.1 5.9 collective-permute-start.9
  179.1 10.6 collective-permute-start.10
  180.0 13.3 collective-permute-start.11
  189.7 14.9 collective-permute-start.12
  193.4 14.8 collective-permute-start.13
  204.7 5.9 collective-permute-start.14
  249.9 9.8 copy-start.20
  291.9 110.1 %copy-start.8 = (f32[128,16,64]{0,2,1:T(8,128)}, f32[128,16,64]{0,2,1:T(8,128)S(1)}, u32[]{:S(2)}) copy-start(f32[128,16,64]{0,2,1:T(8,128)S(1)} %get-tuple-element.154) | copy-start | bytes 1572868
  292.0 110.0 %copy-start.6 = (bf16[128,16,64]{0,2,1:T(8,128)(2,1)}, bf16[128,16,64]{0,2,1:T(8,128)(2,1)S(1)}, u32[]{:S(2)}) copy-start(bf16[128,16,64]{0,2,1:T(8,128)(2,1)S(1)} %fusion.85) | copy-start | bytes 786436
  391.8 78.5 %copy-start.10 = (bf16[128,1024]{1,0:T(8,128)(2,1)S(1)}, bf16[128,1024]{1,0:T(8,128)(2,1)}, u32[]{:S(2)}) copy-start(bf16[128,1024]{1,0:T(8,128)(2,1)} %param.31) | copy-start | bytes 786436
  493.0 3.6 copy-start.9
  498.1 3.4 copy-start.5
  498.1 3.4 copy-start.14
  501.2 7.5 copy-start.3
  508.7 4.0 copy-start.2
  512.7 4.1 copy-start.4
  512.7 4.1 copy-start.15
  521.1 3.4 copy-start.5
  521.2 3.4 copy-start.14
  524.3 7.5 copy-start.3
  531.8 4.0 copy-start.2
  535.8 4.1 copy-start.4
  535.8 4.1 copy-start.15
  566.9 145.5 %reduce-scatter.21.cloned.1.call-start = ((), (), s32[]{:S(2)}) async-start(), calls=%async_computation.20 | async-start | bytes 4456448
  590.3 0.9 copy-start.7
  590.3 261.1 %reduce-scatter.13.cloned.1.call-start = ((), (), s32[]{:S(2)}) async-start(), calls=%async_computation.16 | async-start | bytes 4325376 | tf_op jit(solution)/shard_map/reduce_scatter | solution.py:301
  594.1 119.6 %copy-start.17 = (f32[128,32]{0,1:T(8,128)S(1)}, f32[128,32]{0,1:T(8,128)}, u32[]{:S(2)}) copy-start(f32[128,32]{0,1:T(8,128)} %copy-done.16) | copy-start | bytes 49156
  594.1 119.6 %copy-start.19 = (f32[128,32]{0,1:T(8,128)S(1)}, f32[128,32]{0,1:T(8,128)}, u32[]{:S(2)}) copy-start(f32[128,32]{0,1:T(8,128)} %copy-done.18) | copy-start | bytes 49156
  594.1 120.8 %copy-start.13 = (f32[1024]{0:T(1024)S(1)}, f32[1024]{0:T(1024)}, u32[]{:S(2)}) copy-start(f32[1024]{0:T(1024)} %copy-done.12) | copy-start | bytes 12292
  594.1 120.8 %copy-start.24 = (f32[128]{0:T(128)S(1)}, f32[128]{0:T(128)}, u32[]{:S(2)}) copy-start(f32[128]{0:T(128)} %copy-done.23) | copy-start | bytes 1540
  594.1 419.8 %reduce-scatter.11.cloned.1.call-start = ((), (), s32[]{:S(2)}) async-start(), calls=%async_computation.15 | async-start | bytes 12976128 | tf_op jit(solution)/shard_map/reduce_scatter | solution.py:300
  721.3 1.0 copy-start.11
  721.3 479.9 %reduce-scatter.17.cloned.1.call-start = ((), (), s32[]{:S(2)}) async-start(), calls=%async_computation.18 | async-start | bytes 17301504 | tf_op jit(solution)/shard_map/reduce_scatter | solution.py:303
  730.4 832.4 %reduce-scatter.15.cloned.1.call-start = ((), (), s32[]{:S(2)}) async-start(), calls=%async_computation.17 | async-start | bytes 34603008 | tf_op jit(solution)/shard_map/reduce_scatter | solution.py:302
  745.3 0.7 copy-start.26
  752.1 53.0 %all-to-all-start.2 = ((bf16[16,8,1024]{2,1,0:T(8,128)(2,1)}), bf16[16,8,1024]{2,1,0:T(8,128)(2,1)S(1)}, u32[]{:S(2)}, u32[]{:S(2)}) async-start(bf16[16,8,1024]{2,1,0:T(8,128)(2,1)} %fusion.84), calls=%async_computation.2 | async-start | bytes 524288 | tf_op jit(solution)/shard_map/all_to_all | solution.py:311
  757.4 5.4 copy-start.25
  757.4 805.3 %copy-start.1 = (bf16[128,1024]{1,0:T(8,128)(2,1)S(1)}, bf16[128,1024]{1,0:T(8,128)(2,1)}, u32[]{:S(2)}) copy-start(bf16[128,1024]{1,0:T(8,128)(2,1)} %param.19) | copy-start | bytes 786436
Sparse Core Ops, SparseCore 0:
  10.9 74.3 all-gather.8
  93.2 59.3 all-gather.10
  155.4 62.4 all-gather.18
  220.6 54.7 all-gather.12
  278.1 113.7 all-gather.14
  394.6 75.7 all-gather.16
  567.1 69.5 reduce-scatter.18
  641.0 71.4 reduce-scatter.20
  715.3 136.0 reduce-scatter.12
  857.8 156.0 reduce-scatter.10
  1016.9 184.3 reduce-scatter.16
  1204.1 358.6 reduce-scatter.14
